TPU v7x, 512 devices: a whole 4x4x16 slice. The times are simulated.
512 devices in a mesh: leaf: 32 (over y, x, core), col: 16 (over z).
Axes of the slice: x: 4, y: 4, z: 16, core: 2. Of those that a mesh axis runs over, the one named last changes fastest.
Arguments:
- histograms: bfloat16 [4, 128, 1024, 512], P(None, 'leaf', 'col'), may hold values from -6 to 6
- diag_inv: bfloat16 [4, 128, 512, 512], P(None, 'leaf', 'col'), as said below
- below_panel: bfloat16 [4, 128, 256, 512], P(None, 'leaf', 'col'), may hold values from -0.1875 to 0.1875
- parent_map: int32 [3, 128], P(None, 'leaf'), may hold values from 0 to 127, as said below
- row_lists: int32 [3, 128, 256], P(None, 'leaf'), may hold values from 0 to 511, as said below
Outputs:
- solution: bfloat16 [4, 128, 1024, 512], P(None, 'leaf', 'col')
- upward: bfloat16 [128, 1024, 256], P('leaf', 'col')
Inputs may be any that keep to these rules, and one draw needn't show every extreme that they name: `parent_map`: entry [l, j] names a supernode of tier l + 1 whose owner (index // 4) is the owner of supernode j (j // 4) or the leaf index that differs from it in bit l mod log2(32); at every tier some leaf index sends all its updates to that other index. `row_lists`: the 256 entries of each list are distinct. `diag_inv`: every block is lower triangular with a positive diagonal.
All inputs are finite; a program needn't handle non-finite values.
Results may differ from a plain program's by a relative error of at most 0.012.
Values may be sent and summed in bfloat16 or wider, within the bound.
A program may use at most 64 MiB of HBM per device.

v0:
```python
import jax
import jax.numpy as jnp
from jax import lax
from jax.sharding import PartitionSpec as P


def swapped(block, axis, apart):
    count = lax.axis_size(axis)
    route = []
    for low in range(count):
        high = low | 1 << apart
        if high != low and high < count:
            route += [(low, high), (high, low)]
    return lax.ppermute(block, axis, route)


def spread_rows(update, lists, slots, per_device, node_width):
    slot_match = (
        slots[:, None, None, None] == jnp.arange(per_device, dtype=jnp.int32)[None, None, :, None]
    )
    row_match = (
        lists[:, :, None, None] == jnp.arange(node_width, dtype=jnp.int32)[None, None, None, :]
    )
    placing = jnp.logical_and(slot_match, row_match).astype(jnp.bfloat16)
    upper_part = update.astype(jnp.bfloat16)
    lower_part = (update - upper_part.astype(jnp.float32)).astype(jnp.bfloat16)
    first = jnp.einsum("scr,srpw->pcw", upper_part, placing, preferred_element_type=jnp.float32)
    second = jnp.einsum("scr,srpw->pcw", lower_part, placing, preferred_element_type=jnp.float32)
    return first + second


def route(update, targets, lists, bit_number, myself, per_device, node_width):
    owners = targets // per_device
    slots = targets % per_device
    staying = owners == myself
    self_slots = jnp.where(staying, slots, -1)
    peer_slots = jnp.where(staying, -1, slots)
    kept = spread_rows(update, lists, self_slots, per_device, node_width)
    leaving = spread_rows(update, lists, peer_slots, per_device, node_width)
    arrived = swapped(leaving.astype(jnp.bfloat16), "leaf", bit_number).astype(leaving.dtype)
    return kept + arrived


def on_device(histograms, diag_inv, below_panel, parent_map, row_lists):
    tier_count = histograms.shape[0]
    per_device = histograms.shape[1]
    node_width = histograms.shape[3]
    bit_count = max(lax.axis_size("leaf").bit_length() - 1, 1)
    myself = lax.axis_index("leaf")
    incoming = jnp.zeros(histograms.shape[1:], jnp.float32)
    solved = []
    upward = None
    for height in range(tier_count):
        source = (histograms[height].astype(jnp.float32) - incoming).astype(jnp.bfloat16)
        result = jnp.einsum(
            "scw,svw->scv",
            source,
            lax.all_gather(diag_inv[height], "col", axis=1, tiled=True),
            preferred_element_type=jnp.float32,
        )
        answer = result.astype(jnp.bfloat16)
        solved.append(answer)
        update = jnp.einsum(
            "scw,srw->scr",
            answer,
            lax.all_gather(below_panel[height], "col", axis=1, tiled=True),
            preferred_element_type=jnp.float32,
        )
        if height == tier_count - 1:
            upward = update.astype(jnp.bfloat16)
        else:
            incoming = route(
                update,
                parent_map[height],
                row_lists[height],
                height % bit_count,
                myself,
                per_device,
                node_width,
            )
    return (jnp.stack(solved), upward)


def solution(mesh):
    return jax.shard_map(
        on_device,
        mesh=mesh,
        in_specs=(
            P(None, "leaf", "col", None),
            P(None, "leaf", "col", None),
            P(None, "leaf", "col", None),
            P(None, "leaf"),
            P(None, "leaf", None),
        ),
        out_specs=(P(None, "leaf", "col", None), P("leaf", "col", None)),
        check_vma=False,
    )
```

profile of v0, /device:TPU:24, one launch (start us, length us, event | category | flops | bytes accessed | tf_op | source)
XLA Modules:
  0.0 591.8 jit_solution(14267621176599889509)
XLA Ops:
  7.2 0.0 all-gather.17.cloned.1.call-start
  7.2 1.9 fusion.83
  9.1 0.0 all-gather.17.cloned.1.call-update
  9.1 0.0 all-gather.19.cloned.1.call-start
  9.2 1.6 fusion.84
  10.8 0.0 all-gather.19.cloned.1.call-update
  10.8 0.0 all-gather.21.cloned.1.call-start
  10.9 0.7 all-gather.21.cloned.1.call-update
  11.6 0.0 all-gather.23.cloned.1.call-start
  11.6 0.5 all-gather.23.cloned.1.call-update
  12.2 0.0 all-gather.25.cloned.1.call-start
  12.2 0.5 all-gather.25.cloned.1.call-update
  12.7 0.0 all-gather.27.cloned.1.call-start
  12.8 0.5 all-gather.27.cloned.1.call-update
  13.3 0.0 all-gather.29.cloned.1.call-start
  13.4 0.7 all-gather.29.cloned.1.call-update
  14.1 0.0 all-gather.31.cloned.1.call-start
  14.1 0.7 all-gather.31.cloned.1.call-update
  14.8 0.4 iota_compare_fusion.2
  15.3 0.1 iota_compare_fusion.7
  15.3 5.1 broadcast_and_fusion.5
  20.5 5.5 copy.10
  26.0 0.1 iota_compare_fusion.5
  26.1 0.1 iota_compare_fusion.4
  26.2 0.7 iota_compare_fusion
  26.9 5.4 broadcast_and_fusion.3
  32.3 55.7 %all-gather.17.cloned.1.call-done = bf16[1,4,512,512]{3,2,1,0:T(8,128)(2,1)} async-done(((bf16[1,4,32,512]{3,2,1,0:T(8,128)(2,1)}), bf16[1,4,512,512]{3,2,1,0:T(8,128)(2,1)}) %all-gather.17.cloned.1.call-update) | async-done | bytes 2097168 | tf_op jit(solution)/shard_map/all_gather | solution.py:58
  87.9 2.4 fusion.20
  90.4 67.6 %all-gather.19.cloned.1.call-done = bf16[1,4,256,512]{3,2,1,0:T(8,128)(2,1)} async-done(((bf16[1,4,16,512]{3,2,1,0:T(8,128)(2,1)}), bf16[1,4,256,512]{3,2,1,0:T(8,128)(2,1)}) %all-gather.19.cloned.1.call-update) | async-done | bytes 1048592 | tf_op jit(solution)/shard_map/all_gather | solution.py:66
  157.9 1.7 fusion.40
  159.6 1.4 convolution_bitcast_fusion.8
  161.0 1.4 fusion.32
  162.4 2.1 collective-permute-start
  164.5 0.1 iota_compare_fusion.3
  164.6 5.5 copy.7
  170.1 5.5 copy.16
  175.7 2.2 convolution_bitcast_fusion.10
  177.8 51.9 %all-gather.21.cloned.1.call-done = bf16[1,4,512,512]{3,2,1,0:T(8,128)(2,1)} async-done(((bf16[1,4,32,512]{3,2,1,0:T(8,128)(2,1)}), bf16[1,4,512,512]{3,2,1,0:T(8,128)(2,1)}) %all-gather.21.cloned.1.call-update) | async-done | bytes 2097168 | tf_op jit(solution)/shard_map/all_gather | solution.py:58
  229.7 0.0 collective-permute-done
  229.7 4.6 fusion.23
  234.3 65.1 %all-gather.23.cloned.1.call-done = bf16[1,4,256,512]{3,2,1,0:T(8,128)(2,1)} async-done(((bf16[1,4,16,512]{3,2,1,0:T(8,128)(2,1)}), bf16[1,4,256,512]{3,2,1,0:T(8,128)(2,1)}) %all-gather.23.cloned.1.call-update) | async-done | bytes 1048592 | tf_op jit(solution)/shard_map/all_gather | solution.py:66
  299.4 1.7 fusion.38
  301.1 1.4 convolution_bitcast_fusion.4
  302.5 2.1 fusion.33
  304.6 3.6 collective-permute-start.1
  308.2 5.2 broadcast_and_fusion.1
  313.4 5.5 copy.13
  318.9 5.5 copy.22
  324.4 2.2 convolution_bitcast_fusion.6
  326.6 44.5 %all-gather.25.cloned.1.call-done = bf16[1,4,512,512]{3,2,1,0:T(8,128)(2,1)} async-done(((bf16[1,4,32,512]{3,2,1,0:T(8,128)(2,1)}), bf16[1,4,512,512]{3,2,1,0:T(8,128)(2,1)}) %all-gather.25.cloned.1.call-update) | async-done | bytes 2097168 | tf_op jit(solution)/shard_map/all_gather | solution.py:58
  371.1 0.0 collective-permute-done.1
  371.1 4.6 fusion.26
  375.7 65.6 %all-gather.27.cloned.1.call-done = bf16[1,4,256,512]{3,2,1,0:T(8,128)(2,1)} async-done(((bf16[1,4,16,512]{3,2,1,0:T(8,128)(2,1)}), bf16[1,4,256,512]{3,2,1,0:T(8,128)(2,1)}) %all-gather.27.cloned.1.call-update) | async-done | bytes 1048592 | tf_op jit(solution)/shard_map/all_gather | solution.py:66
  441.3 1.7 fusion.36
  442.9 1.4 convolution_bitcast_fusion
  444.3 1.4 fusion.34
  445.7 4.9 collective-permute-start.2
  450.6 5.5 copy.19
  456.2 2.2 convolution_bitcast_fusion.2
  458.4 54.6 %all-gather.29.cloned.1.call-done = bf16[1,4,512,512]{3,2,1,0:T(8,128)(2,1)} async-done(((bf16[1,4,32,512]{3,2,1,0:T(8,128)(2,1)}), bf16[1,4,512,512]{3,2,1,0:T(8,128)(2,1)}) %all-gather.29.cloned.1.call-update) | async-done | bytes 2097168 | tf_op jit(solution)/shard_map/all_gather | solution.py:58
  513.0 3.9 fusion.29
  516.9 1.1 pad_maximum_fusion
  518.0 64.6 %all-gather.31.cloned.1.call-done = bf16[1,4,256,512]{3,2,1,0:T(8,128)(2,1)} async-done(((bf16[1,4,16,512]{3,2,1,0:T(8,128)(2,1)}), bf16[1,4,256,512]{3,2,1,0:T(8,128)(2,1)}) %all-gather.31.cloned.1.call-update) | async-done | bytes 1048592 | tf_op jit(solution)/shard_map/all_gather | solution.py:66
  582.7 2.3 convolution_convert_fusion
  (21 shorter events, 0.1 us)
Async XLA Ops:
  7.2 7.7 %copy-start.6 = (s32[3,4,256]{2,1,0:T(4,128)S(1)}, s32[3,4,256]{2,1,0:T(4,128)}, u32[]{:S(2)}) copy-start(s32[3,4,256]{2,1,0:T(4,128)} %param.9) | copy-start | bytes 36868
  7.2 8.0 %copy-start.7 = (s32[3,4]{1,0:T(4,128)S(1)}, s32[3,4]{1,0:T(4,128)}, u32[]{:S(2)}) copy-start(s32[3,4]{1,0:T(4,128)} %param.8) | copy-start | bytes 148
  7.2 80.7 %all-gather.17.cloned.1.call-start = ((), (), s32[]{:S(2)}) async-start(), calls=%async_computation | async-start | bytes 2228224 | tf_op jit(solution)/shard_map/all_gather | solution.py:58
  9.1 148.8 %all-gather.19.cloned.1.call-start = ((), (), s32[]{:S(2)}) async-start(), calls=%async_computation.1 | async-start | bytes 1114112 | tf_op jit(solution)/shard_map/all_gather | solution.py:66
  10.8 218.9 %all-gather.21.cloned.1.call-start = ((), (), s32[]{:S(2)}) async-start(), calls=%async_computation.2 | async-start | bytes 2228224 | tf_op jit(solution)/shard_map/all_gather | solution.py:58
  11.6 287.8 %all-gather.23.cloned.1.call-start = ((), (), s32[]{:S(2)}) async-start(), calls=%async_computation.3 | async-start | bytes 1114112 | tf_op jit(solution)/shard_map/all_gather | solution.py:66
  12.2 359.0 %all-gather.25.cloned.1.call-start = ((), (), s32[]{:S(2)}) async-start(), calls=%async_computation.4 | async-start | bytes 2228224 | tf_op jit(solution)/shard_map/all_gather | solution.py:58
  12.7 428.5 %all-gather.27.cloned.1.call-start = ((), (), s32[]{:S(2)}) async-start(), calls=%async_computation.5 | async-start | bytes 1114112 | tf_op jit(solution)/shard_map/all_gather | solution.py:66
  13.3 499.7 %all-gather.29.cloned.1.call-start = ((), (), s32[]{:S(2)}) async-start(), calls=%async_computation.6 | async-start | bytes 2228224 | tf_op jit(solution)/shard_map/all_gather | solution.py:58
  14.1 568.6 %all-gather.31.cloned.1.call-start = ((), (), s32[]{:S(2)}) async-start(), calls=%async_computation.7 | async-start | bytes 1114112 | tf_op jit(solution)/shard_map/all_gather | solution.py:66
  161.0 3.6 copy-start.3
  162.4 67.3 %collective-permute-start = (bf16[4,64,512]{2,1,0:T(8,128)(2,1)S(1)}, bf16[4,64,512]{2,1,0:T(8,128)(2,1)}, u32[]{:S(2)}, u32[]{:S(2)}) collective-permute-start(bf16[4,64,512]{2,1,0:T(8,128)(2,1)S(1)} %fusion.32), channel_id=1, source_target_pairs={{0,16},{16,0},{32,48},{48,32},{64,80},{80,64},{96,112},{112,96},{1... | collective-permute-start | bytes 786440 | tf_op jit(solution)/shard_map/ppermute | solution.py:14
  164.6 5.5 copy-start.5
  170.1 5.5 copy-start
  304.6 66.5 %collective-permute-start.1 = (bf16[4,64,512]{2,1,0:T(8,128)(2,1)}, bf16[4,64,512]{2,1,0:T(8,128)(2,1)}, u32[]{:S(2)}, u32[]{:S(2)}) collective-permute-start(bf16[4,64,512]{2,1,0:T(8,128)(2,1)} %fusion.33), channel_id=1, source_target_pairs={{0,32},{32,0},{16,48},{48,16},{64,96},{96,64},{80,112},{112,80},{1... | collective-permute-start | bytes 786440 | tf_op jit(solution)/shard_map/ppermute | solution.py:14
  308.2 5.2 copy-start.2
  318.9 5.5 copy-start.1
  444.3 6.3 %copy-start.4 = (pred[4,256,4,512]{3,2,1,0:T(4,128)(4,1)S(1)}, pred[4,256,4,512]{3,2,1,0:T(4,128)(4,1)}, u32[]{:S(2)}) copy-start(pred[4,256,4,512]{3,2,1,0:T(4,128)(4,1)} %get-tuple-element.11) | copy-start | bytes 6291460
  445.7 67.3 %collective-permute-start.2 = (bf16[4,64,512]{2,1,0:T(8,128)(2,1)S(1)}, bf16[4,64,512]{2,1,0:T(8,128)(2,1)}, u32[]{:S(2)}, u32[]{:S(2)}) collective-permute-start(bf16[4,64,512]{2,1,0:T(8,128)(2,1)S(1)} %fusion.34), channel_id=1, source_target_pairs={{0,64},{64,0},{16,80},{80,16},{32,96},{96,32},{48,112},{112,48},{1... | collective-permute-start | bytes 786440 | tf_op jit(solution)/shard_map/ppermute | solution.py:14
Sparse Core Ops, SparseCore 0:
  10.7 77.2 all-gather.16
  90.6 67.3 all-gather.18
  160.0 69.6 all-gather.20
  231.7 67.7 all-gather.22
  301.4 69.7 all-gather.24
  373.1 68.1 all-gather.26
  443.4 69.5 all-gather.28
  515.1 67.5 all-gather.30
where the time goes:
time: 593 us; the launch traced here: 592 us
  waiting for transfers between devices  473 us (80%)
  matrix products  38.5 us (6%)
  local copies, waits for them, and re-layouts  36.6 us (6%)
  other arithmetic  18.2 us (3%)
  between operations  14.4 us (2%)
  starting transfers between devices  10.9 us (2%)
    all_gather x4, waiting for transfers between devices, on_device(): lax.all_gather(below_panel[height], 'col', axis=1, tiled=True)  263 us
    all_gather x4, waiting for transfers between devices, on_device(): lax.all_gather(diag_inv[height], 'col', axis=1, tiled=True)  207 us
    and x6, local copies, waits for them, and re-layouts, spread_rows(): placing = jnp.logical_and(slot_match, row_match).astype(jnp.bfloat16)  33.1 us
    and x3, other arithmetic, spread_rows(): placing = jnp.logical_and(slot_match, row_match).astype(jnp.bfloat16)  15.7 us
    dot_general x4, matrix products, on_device(): jnp.einsum('scw,svw->scv', source, lax.all_gather(diag_inv[height], 'col'...  15.5 us
  transfers between devices with their start and end apart: 11, of which 8 were waited for; matrix products, arithmetic and copies ran while one was open for 15% of the time, Pallas kernels for 0%

commit v1 on v0

v1 whole, which is shorter than its diff:
```python
import functools
import jax
import jax.numpy as jnp
from jax import lax
from jax.experimental import pallas as pl
from jax.experimental.pallas import tpu as pltpu
from jax.sharding import PartitionSpec as P

MESH = pl.DeviceIdType.MESH
F32, BF16 = jnp.float32, jnp.bfloat16

RING = 16
TIERS = 4
SLOTS = 4
COLS = 64
WIDTH = 512
ROWS = 256
PIECE = 32
DEPTH = 16
LANES = 128
NARROW = 32

UP_DIAG = (9, 8, 7, 6, 9, 6, 6, 7, 6, 6, 6, 7, 7, 9, 9, 9)
UP_BELOW = (9, 9, 9, 9, 7, 6, 7, 6, 6, 6, 7, 9, 9, 8, 6, 9)
MAX_HOP = 9
PERIOD = 6
SHIFT = 3
LAG = 3
LAST = (TIERS - 1) * PERIOD + SHIFT + MAX_HOP
NT = (((1,), (1,)), ((), ()))


def table(values):
    low = sum((v - 6) << (2 * i) for i, v in enumerate(values[:8]))
    high = sum((v - 6) << (2 * i) for i, v in enumerate(values[8:]))
    return low, high


def hops_up(words, z):
    word = jnp.where(z < 8, jnp.int32(words[0]), jnp.int32(words[1]))
    return 6 + lax.rem(lax.shift_right_logical(word, 2 * lax.rem(z, 8)), 4)


def by_width(z, act, low=0, high=RING):
    if high - low == 1:
        act(high)
        return
    middle = (low + high) // 2

    def lower():
        by_width(z, act, low, middle)

    def upper():
        by_width(z, act, middle, high)

    lax.cond(z < middle, lower, upper)


def kernel(
    hist_hbm, diag_hbm, below_hbm, parent_ref, rows_ref,
    solved_hbm, upward_hbm,
    hist, diag, gathered, panels, spread, answer, kept, leaving, outbox, inbox, top,
    load_sem, diag_send, diag_recv, below_send, below_recv, swap_send, swap_recv, store_sem,
):
    me = lax.axis_index("col")
    leaf = lax.axis_index("leaf")
    above = lax.rem(me + 1, RING)
    under = lax.rem(me + RING - 1, RING)
    ups = table(UP_DIAG), table(UP_BELOW)

    def partner(bit):
        return leaf + (1 << bit) * (1 - 2 * lax.rem(leaf // (1 << bit), 2))

    loads = [
        pltpu.make_async_copy(diag_hbm.at[0], diag.at[0], load_sem.at[0]),
        pltpu.make_async_copy(below_hbm.at[0], panels.at[0, me], load_sem.at[1]),
    ]
    for t in range(1, TIERS):
        loads.append(pltpu.make_async_copy(diag_hbm.at[t], diag.at[t], load_sem.at[2 * t]))
        loads.append(pltpu.make_async_copy(below_hbm.at[t], panels.at[t, me], load_sem.at[2 * t + 1]))
    loads.append(pltpu.make_async_copy(hist_hbm, hist, load_sem.at[2 * TIERS]))
    for load in loads:
        load.start()

    barrier = pltpu.get_barrier_semaphore()
    for ring in (above, under):
        pl.semaphore_signal(barrier, inc=1, device_id={"col": ring}, device_id_type=MESH)
    for bit in range(TIERS - 1):
        pl.semaphore_signal(barrier, inc=1, device_id={"leaf": partner(bit)}, device_id_type=MESH)

    group = lax.broadcasted_iota(jnp.int32, (1, LANES), 1) // NARROW

    def pack(t):
        loads[2 * t].wait()
        loads[2 * t + 1].wait()
        for q in range(WIDTH // LANES):
            wide = [diag[t, s, :, q * LANES:(q + 1) * LANES].astype(F32) for s in range(SLOTS)]
            for a in range(LANES // NARROW):
                tile = jnp.zeros((PIECE, LANES), F32)
                for s in range(SLOTS):
                    turn = NARROW * ((s - a) % 4)
                    moved = pltpu.roll(wide[s], turn, axis=1) if turn else wide[s]
                    tile = jnp.where(group == s, moved, tile)
                gathered[t, me, 4 * q + a] = tile.astype(BF16)

    def gather_diag(direction, t, k):
        z = lax.rem(me - k + RING, RING) if direction == 0 else lax.rem(me + k, RING)
        far = hops_up(ups[0], z)
        if direction:
            far = RING - 1 - far
        target = above if direction == 0 else under

        def act(n):
            block = gathered.at[t, z, pl.ds(0, n)]
            copy = pltpu.make_async_remote_copy(
                src_ref=block, dst_ref=block,
                send_sem=diag_send.at[direction, t, k], recv_sem=diag_recv.at[direction, t, k],
                device_id={"col": target}, device_id_type=MESH,
            )
            arriving = pltpu.make_async_remote_copy(
                src_ref=block, dst_ref=block,
                send_sem=diag_send.at[direction, t, k],
                recv_sem=diag_recv.at[direction, t, jnp.maximum(k - 1, 0)],
                device_id={"col": target}, device_id_type=MESH,
            )

            @pl.when(k >= 1)
            def _():
                arriving.wait_recv()

            @pl.when(k < far)
            def _():
                copy.start()

        @pl.when(k <= far)
        def _():
            by_width(z, act)

    def drain_diag(direction, t, k):
        z = lax.rem(me - k + RING, RING) if direction == 0 else lax.rem(me + k, RING)
        far = hops_up(ups[0], z)
        if direction:
            far = RING - 1 - far
        target = above if direction == 0 else under

        def act(n):
            block = gathered.at[t, z, pl.ds(0, n)]
            pltpu.make_async_remote_copy(
                src_ref=block, dst_ref=block,
                send_sem=diag_send.at[direction, t, k], recv_sem=diag_recv.at[direction, t, k],
                device_id={"col": target}, device_id_type=MESH,
            ).wait_send()

        @pl.when(k < far)
        def _():
            by_width(z, act)

    def below_copy(direction, t, k, landed, z):
        block = panels.at[t, z]
        return pltpu.make_async_remote_copy(
            src_ref=block, dst_ref=block,
            send_sem=below_send.at[direction, t, k], recv_sem=below_recv.at[direction, t, landed],
            device_id={"col": above if direction == 0 else under}, device_id_type=MESH,
        )

    def gather_below(direction, t, k):
        z = lax.rem(me - k + RING, RING) if direction == 0 else lax.rem(me + k, RING)
        far = hops_up(ups[1], z)
        if direction:
            far = RING - 1 - far

        @pl.when(jnp.logical_and(k >= 1, k <= far))
        def _():
            below_copy(direction, t, k, jnp.maximum(k - 1, 0), z).wait_recv()

        @pl.when(k < far)
        def _():
            below_copy(direction, t, k, k, z).start()

    def drain_below(direction, t, k):
        z = lax.rem(me - k + RING, RING) if direction == 0 else lax.rem(me + k, RING)
        far = hops_up(ups[1], z)
        if direction:
            far = RING - 1 - far

        @pl.when(k < far)
        def _():
            below_copy(direction, t, k, k, z).wait_send()

    def swap(t):
        return pltpu.make_async_remote_copy(
            src_ref=outbox.at[t], dst_ref=inbox.at[t],
            send_sem=swap_send.at[t], recv_sem=swap_recv.at[t],
            device_id={"leaf": partner(t)}, device_id_type=MESH,
        )

    def store(t):
        return pltpu.make_async_copy(answer.at[t], solved_hbm.at[t], store_sem.at[t])

    def make_source(t):
        if t == 0:
            loads[2 * TIERS].wait()
        else:
            swap(t - 1).wait()
        for s in range(SLOTS):
            values = hist[t, s].astype(F32)
            if t > 0:
                values = values - (kept[s] + inbox[t - 1, s].astype(F32))
            values = values.astype(BF16).astype(F32)
            for m in range(WIDTH // NARROW):
                q, a = m // 4, m % 4
                tile = values[:, q * LANES:(q + 1) * LANES]
                turn = NARROW * ((s - a) % 4)
                if turn:
                    tile = pltpu.roll(tile, turn, axis=1)
                tile = jnp.where(group == s, tile, 0.0).astype(BF16)
                spread[s * COLS:(s + 1) * COLS, m * LANES:(m + 1) * LANES] = tile

    def solve(t, half):
        tiles = 8 if half == 0 else 16
        columns = []
        for m in range(tiles):
            blocks = []
            for z in range(8 * half, 8 * half + 8):
                blocks.append(gathered[t, z, m] if z >= m else jnp.zeros((PIECE, LANES), BF16))
            columns.append(jnp.concatenate(blocks, axis=0))
        weights = jnp.concatenate(columns, axis=1)
        result = lax.dot_general(spread[:, :tiles * LANES], weights, NT, preferred_element_type=F32)
        result = result.astype(BF16)
        for s in range(SLOTS):
            answer[t, s, :, half * 256:(half + 1) * 256] = result[s * COLS:(s + 1) * COLS]

    def updated(t, s):
        panel = jnp.concatenate([panels[t, z, s] for z in range(RING)], axis=0)
        return lax.dot_general(answer[t, s], panel, NT, preferred_element_type=F32)

    def place(t, s):
        update = updated(t, s)
        upper = update.astype(BF16)
        lower = (update - upper.astype(F32)).astype(BF16)
        both = jnp.concatenate([upper, lower], axis=0)
        wanted = rows_ref[t, s:s + 1, :]
        landing = lax.broadcasted_iota(jnp.int32, (WIDTH, ROWS), 0) == wanted
        landing = landing.astype(F32).astype(BF16)
        placed = lax.dot_general(both, landing, NT, preferred_element_type=F32)
        placed = placed[:COLS] + placed[COLS:]
        parent = parent_ref[t, s]
        owner = parent // SLOTS
        slot = lax.rem(parent, SLOTS)
        stays = owner == leaf
        for p in range(SLOTS):
            here = jnp.where(jnp.logical_and(stays, slot == p), placed, 0.0)
            there = jnp.where(jnp.logical_and(jnp.logical_not(stays), slot == p), placed, 0.0)
            if s == 0:
                kept[p] = here
                leaving[p] = there
            else:
                kept[p] += here
                leaving[p] += there
        if s == SLOTS - 1:
            outbox[t] = leaving[...].astype(BF16)

    pack(0)
    pl.semaphore_wait(barrier, 2 + TIERS - 1)

    plan = {}

    def at(slot, unit):
        plan.setdefault(slot, []).append(unit)

    for t in range(1, TIERS):
        at(t - 1, functools.partial(pack, t))
    for t in range(TIERS):
        ready = t * PERIOD + MAX_HOP + (1 if t else 0)

        def first(t=t):
            make_source(t)
            solve(t, 0)

        def second(t=t):
            solve(t, 1)
            store(t).start()

        at(ready, first)
        at(ready + 1, second)
        whole = t * PERIOD + SHIFT + MAX_HOP
        if t < TIERS - 1:
            for s in range(2):
                at(whole, functools.partial(place, t, s))
            for s in range(2, 4):
                at(whole + 1, functools.partial(place, t, s))
            at(whole + 2, lambda t=t: swap(t).start())

    def step(slot, carry):
        for ago in (1, 0):
            t = slot // PERIOD - ago
            k = slot - PERIOD * t
            for direction in range(2):
                @pl.when(jnp.logical_and(jnp.logical_and(t >= 0, t < TIERS), k <= MAX_HOP))
                def _():
                    gather_diag(direction, t, k)

            @pl.when(jnp.logical_and(jnp.logical_and(t >= 0, t < TIERS), jnp.logical_and(k >= LAG, k < LAG + MAX_HOP)))
            def _():
                for direction in range(2):
                    drain_diag(direction, t, k - LAG)
        for ago in (1, 0):
            later = slot - SHIFT + PERIOD
            t = later // PERIOD - 1 - ago
            k = later - PERIOD * (t + 1)
            for direction in range(2):
                @pl.when(jnp.logical_and(jnp.logical_and(t >= 0, t < TIERS), k <= MAX_HOP))
                def _():
                    gather_below(direction, t, k)

            @pl.when(jnp.logical_and(jnp.logical_and(t >= 0, t < TIERS), jnp.logical_and(k >= LAG, k < LAG + MAX_HOP)))
            def _():
                for direction in range(2):
                    drain_below(direction, t, k - LAG)
        for when, units in plan.items():
            @pl.when(slot == when)
            def _():
                for unit in units:
                    unit()
        return carry

    lax.fori_loop(0, LAST + 1, step, 0)
    for s in range(SLOTS):
        top[s] = updated(TIERS - 1, s).astype(BF16)
    last = pltpu.make_async_copy(top, upward_hbm, store_sem.at[TIERS])
    last.start()

    def finish(slot, carry):
        for ago in (1, 0):
            later = slot - SHIFT + PERIOD
            t = later // PERIOD - 1 - ago
            k = later - PERIOD * (t + 1)

            @pl.when(jnp.logical_and(jnp.logical_and(t >= 0, t < TIERS), jnp.logical_and(k >= LAG, k < LAG + MAX_HOP)))
            def _():
                for direction in range(2):
                    drain_below(direction, t, k - LAG)
        return carry

    lax.fori_loop(LAST + 1, LAST + LAG, finish, 0)
    for t in range(TIERS):
        store(t).wait()
    last.wait()


def on_device(histograms, diag_inv, below_panel, parent_map, row_lists):
    vmem = pltpu.VMEM
    dma = pltpu.SemaphoreType.DMA
    return pl.pallas_call(
        kernel,
        out_shape=(
            jax.ShapeDtypeStruct((TIERS, SLOTS, COLS, WIDTH), BF16),
            jax.ShapeDtypeStruct((SLOTS, COLS, ROWS), BF16),
        ),
        in_specs=[
            pl.BlockSpec(memory_space=pl.ANY),
            pl.BlockSpec(memory_space=pl.ANY),
            pl.BlockSpec(memory_space=pl.ANY),
            pl.BlockSpec(memory_space=pltpu.SMEM),
            pl.BlockSpec(memory_space=pltpu.VMEM),
        ],
        out_specs=(pl.BlockSpec(memory_space=pl.ANY), pl.BlockSpec(memory_space=pl.ANY)),
        scratch_shapes=[
            vmem((TIERS, SLOTS, COLS, WIDTH), BF16),
            vmem((TIERS, SLOTS, PIECE, WIDTH), BF16),
            vmem((TIERS, RING, RING, PIECE, LANES), BF16),
            vmem((TIERS, RING, SLOTS, DEPTH, WIDTH), BF16),
            vmem((SLOTS * COLS, RING * LANES), BF16),
            vmem((TIERS, SLOTS, COLS, WIDTH), BF16),
            vmem((SLOTS, COLS, WIDTH), F32),
            vmem((SLOTS, COLS, WIDTH), F32),
            vmem((TIERS - 1, SLOTS, COLS, WIDTH), BF16),
            vmem((TIERS - 1, SLOTS, COLS, WIDTH), BF16),
            vmem((SLOTS, COLS, ROWS), BF16),
            dma((2 * TIERS + 1,)),
            dma((2, TIERS, MAX_HOP + 1)),
            dma((2, TIERS, MAX_HOP + 1)),
            dma((2, TIERS, MAX_HOP + 1)),
            dma((2, TIERS, MAX_HOP + 1)),
            dma((TIERS - 1,)),
            dma((TIERS - 1,)),
            dma((TIERS + 1,)),
        ],
        compiler_params=pltpu.CompilerParams(
            collective_id=0, has_side_effects=True, vmem_limit_bytes=60 << 20
        ),
    )(histograms, diag_inv, below_panel, parent_map, row_lists)


def solution(mesh):
    return jax.shard_map(
        on_device,
        mesh=mesh,
        in_specs=(
            P(None, "leaf", "col", None),
            P(None, "leaf", "col", None),
            P(None, "leaf", "col", None),
            P(None, "leaf"),
            P(None, "leaf", None),
        ),
        out_specs=(P(None, "leaf", "col", None), P("leaf", "col", None)),
        check_vma=False,
    )
```

time: 593 us -> 154 us (0.26)
  waiting for transfers between devices: 473 us -> 0 us
  Pallas kernels: 0 us -> 150 us
  matrix products: 38.5 us -> 0 us
  local copies, waits for them, and re-layouts: 36.6 us -> 2.98 us
  other arithmetic: 18.2 us -> 0 us
  between operations: 14.4 us -> 0.65 us
  starting transfers between devices: 10.9 us -> 0 us
    all_gather x8 -> x0, waiting for transfers between devices: 470 us -> none  [the longest x4 263 us: on_device(): lax.all_gather(below_panel[height], 'col', axis=1, tiled=True)]
    pallas_call x0 -> x1, Pallas kernels: none -> 150 us  [on_device(): pl.pallas_call(kernel, out_shape=(jax.ShapeDtypeStruct((TIERS, SLOTS, COL...]
    dot_general x17 -> x0, matrix products: 38.5 us -> none  [the longest x4 15.5 us: on_device(): jnp.einsum('scw,svw->scv', source, lax.all_gather(diag_inv[height], 'col'...]
    and x6 -> x0, local copies, waits for them, and re-layouts: 33.1 us -> none  [spread_rows(): placing = jnp.logical_and(slot_match, row_match).astype(jnp.bfloat16)]
    and x3 -> x0, other arithmetic: 15.7 us -> none  [spread_rows(): placing = jnp.logical_and(slot_match, row_match).astype(jnp.bfloat16)]
    ppermute x3 -> x0, starting transfers between devices: 10.6 us -> none  [swapped(): return lax.ppermute(block, axis, route)]
  transfers between devices with their start and end apart: 11 -> 0, of which waited for: 8 -> 0; matrix products, arithmetic and copies ran while one was open for 15% -> 0% of each run, Pallas kernels for 0% -> 0%
where the time goes in v1:
time: 154 us; the launch traced here: 153 us
  Pallas kernels  150 us (97%)
  local copies, waits for them, and re-layouts  2.98 us (2%)
    pallas_call x1, Pallas kernels, on_device(): pl.pallas_call(kernel, out_shape=(jax.ShapeDtypeStruct((TIERS, SLOTS, COL...  150 us

profile of v1, /device:TPU:24, one launch (start us, length us, event | category | flops | bytes accessed | tf_op | source)
XLA Modules:
  0.0 153.4 jit_solution(8266120909818744859)
XLA Ops:
  0.6 149.8 %shard_map.68 = (bf16[4,4,64,512]{3,2,1,0:T(8,128)(2,1)}, bf16[4,64,256]{2,1,0:T(8,128)(2,1)}) custom-call(bf16[4,4,64,512]{3,2,1,0:T(8,128)(2,1)} %hist_hbm.1, bf16[4,4,32,512]{3,2,1,0:T(8,128)(2,1)} %diag_hbm.1, bf16[4,4,16,512]{3,2,1,0:T(8,128)(2,1)} %below_hbm.1, s32[3,4]{1,0:T(4,128)} %parent_ref.1, s32[3,4,256]{2,1,0:T(4,128)} %rows_ref.1), custom_call_target="tpu_custom_call" | custom-call | tf_op jit(solution)/shard_map/pallas_call | solution.py:354
  150.4 0.0 copy-start
  150.4 2.3 %copy.9 = bf16[4,4,64,512]{3,2,1,0:T(8,128)(2,1)} copy(bf16[4,4,64,512]{3,2,1,0:T(8,128)(2,1)} %get-tuple-element.4) | data formatting | bytes 2097152
  152.8 0.0 copy-done
  152.8 0.7 copy.10
Async XLA Ops:
  150.4 2.3 %copy-start = (bf16[4,64,256]{2,1,0:T(8,128)(2,1)S(1)}, bf16[4,64,256]{2,1,0:T(8,128)(2,1)}, u32[]{:S(2)}) copy-start(bf16[4,64,256]{2,1,0:T(8,128)(2,1)} %get-tuple-element.5) | copy-start | bytes 393220

commit v2 on v1

v2 whole, which is shorter than its diff:
```python
import functools
import jax
import jax.numpy as jnp
from jax import lax
from jax.experimental import pallas as pl
from jax.experimental.pallas import tpu as pltpu
from jax.sharding import PartitionSpec as P

MESH = pl.DeviceIdType.MESH
F32, BF16 = jnp.float32, jnp.bfloat16

RING = 16
TIERS = 4
SLOTS = 4
COLS = 64
WIDTH = 512
ROWS = 256
PIECE = 32
DEPTH = 16
LANES = 128
NARROW = 32

HOPS_UP = (
    (9, 8, 6, 7, 7, 6, 6, 7, 6, 6, 7, 9, 9, 6, 9, 9),
    (9, 8, 10, 9, 6, 5, 8, 9, 7, 7, 8, 8, 8, 7, 8, 8),
    (10, 10, 10, 6, 9, 8, 6, 6, 6, 6, 5, 5, 10, 8, 10, 10),
)
PIECES = (
    (0, 0, 0),
    (1, 2, 0),
    (0, 1, 1),
    (2, 1, 7),
    (3, 2, 10),
    (3, 1, 11),
    (2, 2, 5),
    (1, 1, 4),
    (0, 2, 0),
    (3, 0, 9),
    (2, 0, 5),
    (1, 0, 2),
)
MAX_HOP = 10
REACH = tuple(
    max(max(r, 15 - r) for r in (up[8:] if piece == 1 else up)) for piece, up in enumerate(HOPS_UP)
)
LAG = 6
LAST = max(start + REACH[piece] for _, piece, start in PIECES)
HALF = RING // 2
SWAP_SLOTS = (1, 2, 2)
NT = (((1,), (1,)), ((), ()))


def table(values):
    low = sum((v - 5) << (3 * i) for i, v in enumerate(values[:8]))
    high = sum((v - 5) << (3 * i) for i, v in enumerate(values[8:]))
    return low, high


def hops_up(words, z):
    word = jnp.where(z < 8, jnp.int32(words[0]), jnp.int32(words[1]))
    return 5 + lax.rem(lax.shift_right_logical(word, 3 * lax.rem(z, 8)), 8)


def by_width(w, act, low=0, high=HALF):
    if high - low == 1:
        act(high)
        return
    middle = (low + high) // 2

    def lower():
        by_width(w, act, low, middle)

    def upper():
        by_width(w, act, middle, high)

    lax.cond(w < middle, lower, upper)


def kernel(
    hist_hbm, diag_hbm, below_hbm, parent_ref, rows_ref,
    solved_hbm, upward_hbm,
    hist, diag, gathered, panels, spread, answer, kept, placed, partial, lower, marks, guest_marks, card, guest, sorted_in, outbox, inbox, top,
    load_sem, ring_send, ring_recv, swap_send, swap_recv, card_send, card_recv, store_sem,
):
    me = lax.axis_index("col")
    leaf = lax.axis_index("leaf")
    above = lax.rem(me + 1, RING)
    under = lax.rem(me + RING - 1, RING)
    ups = [table(values) for values in HOPS_UP]

    def partner(bit):
        return leaf + (1 << bit) * (1 - 2 * lax.rem(leaf // (1 << bit), 2))

    loads = [
        pltpu.make_async_copy(diag_hbm.at[0], diag.at[0], load_sem.at[0]),
        pltpu.make_async_copy(below_hbm.at[0], panels.at[0, me], load_sem.at[1]),
    ]
    for t in range(1, TIERS):
        loads.append(pltpu.make_async_copy(diag_hbm.at[t], diag.at[t], load_sem.at[2 * t]))
        loads.append(pltpu.make_async_copy(below_hbm.at[t], panels.at[t, me], load_sem.at[2 * t + 1]))
    loads.append(pltpu.make_async_copy(hist_hbm, hist, load_sem.at[2 * TIERS]))
    for load in loads:
        load.start()

    barrier = pltpu.get_barrier_semaphore()
    for ring in (above, under):
        pl.semaphore_signal(barrier, inc=1, device_id={"col": ring}, device_id_type=MESH)
    for bit in range(TIERS - 1):
        pl.semaphore_signal(barrier, inc=1, device_id={"leaf": partner(bit)}, device_id_type=MESH)

    group = lax.broadcasted_iota(jnp.int32, (1, LANES), 1) // NARROW

    def pack(t):
        loads[2 * t].wait()
        for q in range(WIDTH // LANES):
            wide = [diag[t, s, :, q * LANES:(q + 1) * LANES].astype(F32) for s in range(SLOTS)]
            for a in range(LANES // NARROW):
                tile = jnp.zeros((PIECE, LANES), F32)
                for s in range(SLOTS):
                    turn = NARROW * ((s - a) % 4)
                    moved = pltpu.roll(wide[s], turn, axis=1) if turn else wide[s]
                    tile = jnp.where(group == s, moved, tile)
                gathered[t, me, 4 * q + a] = tile.astype(BF16)

    def aim(direction, piece, k):
        z = lax.rem(me - k + RING, RING) if direction == 0 else lax.rem(me + k, RING)
        far = hops_up(ups[piece], z)
        if direction:
            far = RING - 1 - far
        if piece == 1:
            far = jnp.where(z >= HALF, far, -1)
        return z, far

    def each_block(piece, t, z, act):
        if piece == 2:
            act(panels.at[t, z])
        elif piece == 1:
            by_width(z - HALF, lambda n: act(gathered.at[t, z, pl.ds(HALF, n)]))
        else:
            by_width(jnp.minimum(z, HALF - 1), lambda n: act(gathered.at[t, z, pl.ds(0, n)]))

    def ring_copy(direction, piece, t, block, k, landed):
        return pltpu.make_async_remote_copy(
            src_ref=block, dst_ref=block,
            send_sem=ring_send.at[direction, piece, t, k],
            recv_sem=ring_recv.at[direction, piece, t, landed],
            device_id={"col": above if direction == 0 else under}, device_id_type=MESH,
        )

    def gather(direction, piece, t, k):
        z, far = aim(direction, piece, k)

        def act(block):
            @pl.when(k >= 1)
            def _():
                ring_copy(direction, piece, t, block, k, jnp.maximum(k - 1, 0)).wait_recv()

            @pl.when(k < far)
            def _():
                ring_copy(direction, piece, t, block, k, k).start()

        @pl.when(k <= far)
        def _():
            each_block(piece, t, z, act)

    def drain(direction, piece, t, k):
        z, far = aim(direction, piece, k)

        @pl.when(k < far)
        def _():
            each_block(piece, t, z, lambda block: ring_copy(direction, piece, t, block, k, k).wait_send())

    def swap(t):
        return pltpu.make_async_remote_copy(
            src_ref=outbox.at[t], dst_ref=inbox.at[t],
            send_sem=swap_send.at[t], recv_sem=swap_recv.at[t],
            device_id={"leaf": partner(t)}, device_id_type=MESH,
        )

    def store(t):
        return pltpu.make_async_copy(answer.at[t], solved_hbm.at[t], store_sem.at[t])

    def make_source(t, s):
        if s == 0:
            if t == 0:
                loads[2 * TIERS].wait()
        values = hist[t, s].astype(F32)
        if t > 0:
            values = values - kept[s]
        values = values.astype(BF16).astype(F32)
        for m in range(WIDTH // NARROW):
            q, a = m // 4, m % 4
            tile = values[:, q * LANES:(q + 1) * LANES]
            turn = NARROW * ((s - a) % 4)
            if turn:
                tile = pltpu.roll(tile, turn, axis=1)
            tile = jnp.where(group == s, tile, 0.0).astype(BF16)
            spread[s * COLS:(s + 1) * COLS, m * LANES:(m + 1) * LANES] = tile

    def solve(t, half, part):
        columns = []
        for m in range(HALF * part, HALF * part + HALF):
            blocks = []
            for z in range(HALF * half, HALF * half + HALF):
                blocks.append(gathered[t, z, m] if z >= m else jnp.zeros((PIECE, LANES), BF16))
            columns.append(jnp.concatenate(blocks, axis=0))
        weights = jnp.concatenate(columns, axis=1)
        result = lax.dot_general(
            spread[:, HALF * LANES * part:HALF * LANES * (part + 1)], weights, NT, preferred_element_type=F32
        )
        if half == 1 and part == 0:
            partial[...] = result
            return
        if half == 1:
            result = partial[...] + result
        result = result.astype(BF16)
        for s in range(SLOTS):
            answer[t, s, :, half * 256:(half + 1) * 256] = result[s * COLS:(s + 1) * COLS]
        if half == 1:
            store(t).start()

    def updated(t, s):
        panel = jnp.concatenate([panels[t, z, s] for z in range(RING)], axis=0)
        return lax.dot_general(answer[t, s], panel, NT, preferred_element_type=F32)

    def mark(source, marks, t, s):
        hit = lax.broadcasted_iota(jnp.int32, (WIDTH, ROWS), 0) == source[t, s:s + 1, :ROWS]
        marks[t, :, s * ROWS:(s + 1) * ROWS] = hit.astype(F32).astype(BF16)

    def describe(t):
        card[t, :, :ROWS] = rows_ref[t]
        for s in range(SLOTS):
            card[t, s:s + 1, ROWS:] = jnp.full((1, ROWS), parent_ref[t, s], jnp.int32)

    def introduce(t):
        return pltpu.make_async_remote_copy(
            src_ref=card.at[t], dst_ref=guest.at[t],
            send_sem=card_send.at[t], recv_sem=card_recv.at[t],
            device_id={"leaf": partner(t)}, device_id_type=MESH,
        )

    def update(t, s):
        value = updated(t, s)
        upper = value.astype(BF16)
        outbox[t, s] = upper
        lower[s] = (value - upper.astype(F32)).astype(BF16)

    def place(t, s):
        both = jnp.concatenate([outbox[t, s], lower[s]], axis=0)
        result = lax.dot_general(both, marks[t, :, s * ROWS:(s + 1) * ROWS], NT, preferred_element_type=F32)
        placed[s] = result[:COLS] + result[COLS:]

    def collect(t, p):
        total = jnp.zeros((COLS, WIDTH), F32)
        for s in range(SLOTS):
            total += jnp.where(parent_ref[t, s] == SLOTS * leaf + p, placed[s], 0.0)
        kept[p] = total

    def sort_inbox(t):
        swap(t).wait()
        for s in range(SLOTS):
            values = inbox[t, s].astype(F32)
            parent = guest[t, s:s + 1, ROWS:]
            for p in range(SLOTS):
                mine = jnp.where(parent == SLOTS * leaf + p, values, 0.0)
                sorted_in[p * COLS:(p + 1) * COLS, s * ROWS:(s + 1) * ROWS] = mine.astype(BF16)

    def land(t, half):
        columns = slice(half * 256, half * 256 + 256)
        result = lax.dot_general(sorted_in[...], guest_marks[t, columns], NT, preferred_element_type=F32)
        for p in range(SLOTS):
            kept[p, :, columns] += result[p * COLS:(p + 1) * COLS]

    plan = {}

    def at(slot, unit):
        plan.setdefault(slot, []).append(unit)

    start = {(t, piece): first for t, piece, first in PIECES}
    def first_at(slot):
        return min(i for i, (_, piece, first) in enumerate(PIECES) if first <= slot <= first + REACH[piece])

    for t in range(TIERS):
        early = min(start[t, 0], start[t, 1]) - 2
        if early < 0:
            pack(t)
        else:
            at((early, first_at(early)), functools.partial(pack, t))
        if start[t, 2] < 1:
            loads[2 * t + 1].wait()
        else:
            at((start[t, 2] - 1, first_at(start[t, 2] - 1)), loads[2 * t + 1].wait)
    for t in range(TIERS - 1):
        describe(t)
    pl.semaphore_wait(barrier, 2 + TIERS - 1)
    for t in range(TIERS - 1):
        introduce(t).start()

    places = [
        (slot, i)
        for slot in range(LAST + 1)
        for i, (_, piece, first) in enumerate(PIECES)
        if first <= slot <= first + REACH[piece]
    ]
    rank = {(t, piece): i for i, (t, piece, _) in enumerate(PIECES)}
    here = 0

    def complete(t, *pieces):
        return max((start[t, piece] + REACH[piece], rank[t, piece]) for piece in pieces)

    def enqueue(unit, earliest=(0, 0), apart=1):
        nonlocal here
        while here < len(places) and places[here] < earliest:
            here += 1
        spot = places[here] if here < len(places) else (LAST + 1, 0)
        at(spot, unit)
        here += apart
        return spot

    for t in range(TIERS - 1):
        at(places[4 + 8 * t], introduce(t).wait)
        for s in range(SLOTS):
            at(places[4 + 8 * t + 2 * s], functools.partial(mark, rows_ref, marks, t, s))
            at(places[5 + 8 * t + 2 * s], functools.partial(mark, guest, guest_marks, t, s))
    sent = (0, 0)
    for t in range(TIERS):
        earliest = complete(t, 0, 1)
        if t:
            arrival = (sent[0] + SWAP_SLOTS[t - 1], sent[1])
            enqueue(functools.partial(sort_inbox, t - 1), arrival)
            enqueue(functools.partial(land, t - 1, 0))
            enqueue(functools.partial(land, t - 1, 1))
        for s in range(SLOTS):
            enqueue(functools.partial(make_source, t, s), earliest)
        for half, part in ((0, 0), (1, 0), (1, 1)):
            enqueue(functools.partial(solve, t, half, part))
        if t < TIERS - 1:
            earliest = complete(t, 2)
            for s in range(SLOTS):
                enqueue(functools.partial(update, t, s), earliest)
            sent = enqueue(lambda t=t: swap(t).start())
            for s in range(SLOTS):
                enqueue(functools.partial(place, t, s))
            for p in range(SLOTS):
                enqueue(functools.partial(collect, t, p))

    def serve(slot, receiving):
        for i, (t, piece, first) in enumerate(PIECES):
            k = slot - first
            if receiving:
                @pl.when(jnp.logical_and(k >= 0, k <= REACH[piece]))
                def _():
                    for direction in range(2):
                        gather(direction, piece, t, k)
                    for when, units in plan.items():
                        if when[1] == i and when[0] <= LAST:
                            @pl.when(slot == when[0])
                            def _():
                                for unit in units:
                                    unit()

        for t, piece, first in PIECES:
            k = slot - first - LAG

            @pl.when(jnp.logical_and(k >= 0, k < REACH[piece]))
            def _():
                for direction in range(2):
                    drain(direction, piece, t, k)

    def step(slot, carry):
        serve(slot, True)
        return carry

    lax.fori_loop(0, LAST + 1, step, 0)
    for when in sorted(plan):
        if when[0] > LAST:
            for unit in plan[when]:
                unit()
    for s in range(SLOTS):
        top[s] = updated(TIERS - 1, s).astype(BF16)
    last = pltpu.make_async_copy(top, upward_hbm, store_sem.at[TIERS])
    last.start()

    def finish(slot, carry):
        serve(slot, False)
        return carry

    lax.fori_loop(LAST + 1, LAST + LAG, finish, 0)
    for t in range(TIERS):
        store(t).wait()
    last.wait()


def on_device(histograms, diag_inv, below_panel, parent_map, row_lists):
    vmem = pltpu.VMEM
    dma = pltpu.SemaphoreType.DMA
    return pl.pallas_call(
        kernel,
        out_shape=(
            jax.ShapeDtypeStruct((TIERS, SLOTS, COLS, WIDTH), BF16),
            jax.ShapeDtypeStruct((SLOTS, COLS, ROWS), BF16),
        ),
        in_specs=[
            pl.BlockSpec(memory_space=pl.ANY),
            pl.BlockSpec(memory_space=pl.ANY),
            pl.BlockSpec(memory_space=pl.ANY),
            pl.BlockSpec(memory_space=pltpu.SMEM),
            pl.BlockSpec(memory_space=pltpu.VMEM),
        ],
        out_specs=(pl.BlockSpec(memory_space=pl.ANY), pl.BlockSpec(memory_space=pl.ANY)),
        scratch_shapes=[
            vmem((TIERS, SLOTS, COLS, WIDTH), BF16),
            vmem((TIERS, SLOTS, PIECE, WIDTH), BF16),
            vmem((TIERS, RING, RING, PIECE, LANES), BF16),
            vmem((TIERS, RING, SLOTS, DEPTH, WIDTH), BF16),
            vmem((SLOTS * COLS, RING * LANES), BF16),
            vmem((TIERS, SLOTS, COLS, WIDTH), BF16),
            vmem((SLOTS, COLS, WIDTH), F32),
            vmem((SLOTS, COLS, WIDTH), F32),
            vmem((SLOTS * COLS, 256), F32),
            vmem((SLOTS, COLS, ROWS), BF16),
            vmem((TIERS - 1, WIDTH, SLOTS * ROWS), BF16),
            vmem((TIERS - 1, WIDTH, SLOTS * ROWS), BF16),
            vmem((TIERS - 1, SLOTS, 2 * ROWS), jnp.int32),
            vmem((TIERS - 1, SLOTS, 2 * ROWS), jnp.int32),
            vmem((SLOTS * COLS, SLOTS * ROWS), BF16),
            vmem((TIERS - 1, SLOTS, COLS, ROWS), BF16),
            vmem((TIERS - 1, SLOTS, COLS, ROWS), BF16),
            vmem((SLOTS, COLS, ROWS), BF16),
            dma((2 * TIERS + 1,)),
            dma((2, 3, TIERS, MAX_HOP + 1)),
            dma((2, 3, TIERS, MAX_HOP + 1)),
            dma((TIERS - 1,)),
            dma((TIERS - 1,)),
            dma((TIERS - 1,)),
            dma((TIERS - 1,)),
            dma((TIERS + 1,)),
        ],
        compiler_params=pltpu.CompilerParams(
            collective_id=0, has_side_effects=True, vmem_limit_bytes=60 << 20
        ),
    )(histograms, diag_inv, below_panel, parent_map, row_lists)


def solution(mesh):
    return jax.shard_map(
        on_device,
        mesh=mesh,
        in_specs=(
            P(None, "leaf", "col", None),
            P(None, "leaf", "col", None),
            P(None, "leaf", "col", None),
            P(None, "leaf"),
            P(None, "leaf", None),
        ),
        out_specs=(P(None, "leaf", "col", None), P("leaf", "col", None)),
        check_vma=False,
    )
```

time: 154 us -> 132 us (0.86)
  Pallas kernels: 150 us -> 128 us
    pallas_call x1, Pallas kernels: 150 us -> 128 us  [on_device(): pl.pallas_call(kernel, out_shape=(jax.ShapeDtypeStruct((TIERS, SLOTS, COL...]
where the time goes in v2:
time: 132 us
  Pallas kernels  128 us (97%)
  local copies, waits for them, and re-layouts  2.98 us (2%)
    pallas_call x1, Pallas kernels, on_device(): pl.pallas_call(kernel, out_shape=(jax.ShapeDtypeStruct((TIERS, SLOTS, COL...  128 us
    unnamed x4, local copies, waits for them, and re-layouts  2.98 us

profile of v2, /device:TPU:24, one launch (start us, length us, event | category | flops | bytes accessed | tf_op | source)
XLA Modules:
  0.0 132.1 jit_solution(9216852261840069381)
XLA Ops:
  0.6 128.4 %shard_map.68 = (bf16[4,4,64,512]{3,2,1,0:T(8,128)(2,1)}, bf16[4,64,256]{2,1,0:T(8,128)(2,1)}) custom-call(bf16[4,4,64,512]{3,2,1,0:T(8,128)(2,1)} %hist_hbm.1, bf16[4,4,32,512]{3,2,1,0:T(8,128)(2,1)} %diag_hbm.1, bf16[4,4,16,512]{3,2,1,0:T(8,128)(2,1)} %below_hbm.1, s32[3,4]{1,0:T(4,128)} %parent_ref.1, s32[3,4,256]{2,1,0:T(4,128)} %rows_ref.1), custom_call_target="tpu_custom_call" | custom-call | tf_op jit(solution)/shard_map/pallas_call | solution.py:397
  129.1 0.0 copy-start
  129.1 2.3 %copy.9 = bf16[4,4,64,512]{3,2,1,0:T(8,128)(2,1)} copy(bf16[4,4,64,512]{3,2,1,0:T(8,128)(2,1)} %get-tuple-element.4) | data formatting | bytes 2097152
  131.4 0.0 copy-done
  131.4 0.7 copy.10
Async XLA Ops:
  129.1 2.3 %copy-start = (bf16[4,64,256]{2,1,0:T(8,128)(2,1)S(1)}, bf16[4,64,256]{2,1,0:T(8,128)(2,1)}, u32[]{:S(2)}) copy-start(bf16[4,64,256]{2,1,0:T(8,128)(2,1)} %get-tuple-element.5) | copy-start | bytes 393220

commit v3 on v2

--- a/solution.py
+++ b/solution.py
@@ -44,6 +44,7 @@
     max(max(r, 15 - r) for r in (up[8:] if piece == 1 else up)) for piece, up in enumerate(HOPS_UP)
 )
 LAG = 6
+PHASES = 3
 LAST = max(start + REACH[piece] for _, piece, start in PIECES)
 HALF = RING // 2
 SWAP_SLOTS = (1, 2, 2)
@@ -324,16 +325,16 @@
             at(places[5 + 8 * t + 2 * s], functools.partial(mark, guest, guest_marks, t, s))
     sent = (0, 0)
     for t in range(TIERS):
-        earliest = complete(t, 0, 1)
         if t:
             arrival = (sent[0] + SWAP_SLOTS[t - 1], sent[1])
             enqueue(functools.partial(sort_inbox, t - 1), arrival)
             enqueue(functools.partial(land, t - 1, 0))
             enqueue(functools.partial(land, t - 1, 1))
         for s in range(SLOTS):
-            enqueue(functools.partial(make_source, t, s), earliest)
-        for half, part in ((0, 0), (1, 0), (1, 1)):
-            enqueue(functools.partial(solve, t, half, part))
+            enqueue(functools.partial(make_source, t, s))
+        enqueue(functools.partial(solve, t, 0, 0), complete(t, 0))
+        enqueue(functools.partial(solve, t, 1, 0))
+        enqueue(functools.partial(solve, t, 1, 1), complete(t, 1))
         if t < TIERS - 1:
             earliest = complete(t, 2)
             for s in range(SLOTS):
@@ -344,22 +345,24 @@
             for p in range(SLOTS):
                 enqueue(functools.partial(collect, t, p))
 
-    def serve(slot, receiving):
+    def serve(slot, receiving, low, high):
         for i, (t, piece, first) in enumerate(PIECES):
             k = slot - first
-            if receiving:
+            if receiving and first < high and first + REACH[piece] >= low:
                 @pl.when(jnp.logical_and(k >= 0, k <= REACH[piece]))
                 def _():
                     for direction in range(2):
                         gather(direction, piece, t, k)
                     for when, units in plan.items():
-                        if when[1] == i and when[0] <= LAST:
+                        if when[1] == i and low <= when[0] < high:
                             @pl.when(slot == when[0])
                             def _():
                                 for unit in units:
                                     unit()
 
         for t, piece, first in PIECES:
+            if first + LAG >= high or first + LAG + REACH[piece] <= low:
+                continue
             k = slot - first - LAG
 
             @pl.when(jnp.logical_and(k >= 0, k < REACH[piece]))
@@ -367,11 +370,13 @@
                 for direction in range(2):
                     drain(direction, piece, t, k)
 
-    def step(slot, carry):
-        serve(slot, True)
-        return carry
-
-    lax.fori_loop(0, LAST + 1, step, 0)
+    cuts = [(LAST + 1) * i // PHASES for i in range(PHASES + 1)]
+    for low, high in zip(cuts[:-1], cuts[1:]):
+        def step(slot, carry, low=low, high=high):
+            serve(slot, True, low, high)
+            return carry
+
+        lax.fori_loop(low, high, step, 0)
     for when in sorted(plan):
         if when[0] > LAST:
             for unit in plan[when]:
@@ -382,7 +387,7 @@
     last.start()
 
     def finish(slot, carry):
-        serve(slot, False)
+        serve(slot, False, LAST + 1, LAST + LAG)
         return carry
 
     lax.fori_loop(LAST + 1, LAST + LAG, finish, 0)

time: 132 us -> 132 us (level)
  no operation moved by 1% of the time
where the time goes in v3:
time: 132 us
  Pallas kernels  128 us (97%)
  local copies, waits for them, and re-layouts  2.98 us (2%)
    pallas_call x1, Pallas kernels, on_device(): pl.pallas_call(kernel, out_shape=(jax.ShapeDtypeStruct((TIERS, SLOTS, COL...  128 us
    unnamed x4, local copies, waits for them, and re-layouts  2.98 us

profile of v3, /device:TPU:24, one launch (start us, length us, event | category | flops | bytes accessed | tf_op | source)
XLA Modules:
  0.0 131.6 jit_solution(3791188843689202632)
XLA Ops:
  0.6 127.9 %shard_map.68 = (bf16[4,4,64,512]{3,2,1,0:T(8,128)(2,1)}, bf16[4,64,256]{2,1,0:T(8,128)(2,1)}) custom-call(bf16[4,4,64,512]{3,2,1,0:T(8,128)(2,1)} %hist_hbm.1, bf16[4,4,32,512]{3,2,1,0:T(8,128)(2,1)} %diag_hbm.1, bf16[4,4,16,512]{3,2,1,0:T(8,128)(2,1)} %below_hbm.1, s32[3,4]{1,0:T(4,128)} %parent_ref.1, s32[3,4,256]{2,1,0:T(4,128)} %rows_ref.1), custom_call_target="tpu_custom_call" | custom-call | tf_op jit(solution)/shard_map/pallas_call | solution.py:402
  128.6 0.0 copy-start
  128.6 2.3 %copy.9 = bf16[4,4,64,512]{3,2,1,0:T(8,128)(2,1)} copy(bf16[4,4,64,512]{3,2,1,0:T(8,128)(2,1)} %get-tuple-element.4) | data formatting | bytes 2097152
  130.9 0.0 copy-done
  130.9 0.7 copy.10
Async XLA Ops:
  128.6 2.3 %copy-start = (bf16[4,64,256]{2,1,0:T(8,128)(2,1)S(1)}, bf16[4,64,256]{2,1,0:T(8,128)(2,1)}, u32[]{:S(2)}) copy-start(bf16[4,64,256]{2,1,0:T(8,128)(2,1)} %get-tuple-element.5) | copy-start | bytes 393220
